TPU v7x, 32 devices: a whole 2x2x4 slice. The times are simulated.
32 devices in a mesh: grp: 4 (over y, x), tp: 8 (over z, core).
Axes of the slice: x: 2, y: 2, z: 4, core: 2. Of those that a mesh axis runs over, the one named last changes fastest.
Arguments:
- teacher_in: bfloat16 [192, 8192], P('tp', 'grp'), may hold values from -6 to 6
- teacher_gate: bfloat16 [8192, 28672], P('grp', 'tp'), may hold values from -0.0625 to 0.0625
- teacher_up: bfloat16 [8192, 28672], P('grp', 'tp'), may hold values from -0.0625 to 0.0625
- teacher_down: bfloat16 [28672, 8192], P('tp', 'grp'), may hold values from -0.046875 to 0.046875
- student_in: bfloat16 [192, 4096], P('tp', 'grp'), may hold values from -6 to 6
- student_gate: bfloat16 [4096, 14336], P('grp', 'tp'), may hold values from -0.09375 to 0.09375
- student_up: bfloat16 [4096, 14336], P('grp', 'tp'), may hold values from -0.09375 to 0.09375
- student_down: bfloat16 [14336, 4096], P('tp', 'grp'), may hold values from -0.046875 to 0.046875
- projector: bfloat16 [4096, 4, 2048], P('grp', None, 'tp'), may hold values from -0.09375 to 0.09375
Outputs:
- grad_input: float32 [192, 4096], P('tp', 'grp')
- grad_gate: float32 [4096, 14336], P('grp', 'tp')
- grad_up: float32 [4096, 14336], P('grp', 'tp')
- grad_down: float32 [14336, 4096], P('tp', 'grp')
- grad_projector: float32 [4096, 4, 2048], P('grp', None, 'tp')
All inputs are finite; a program needn't handle non-finite values.
Results may differ from a plain program's by a relative error of at most 0.017.
Values may be sent and summed in bfloat16 or wider, within the bound.
No kernel may reach another device: no remote copies, remote signals or barrier semaphores. Data moves between devices by JAX's collectives and lax.ppermute only.
A program may use at most 192 MiB of HBM per device.

v0:
```python
import jax
import jax.numpy as jnp
from jax import lax
from jax.sharding import PartitionSpec as P


def body(
    teacher_in,
    teacher_gate,
    teacher_up,
    teacher_down,
    student_in,
    student_gate,
    student_up,
    student_down,
    projector,
):
    bf = jnp.bfloat16
    fl = jnp.float32
    teacher_pair = jnp.concatenate([teacher_gate, teacher_up], axis=1)
    teacher_width = teacher_gate.shape[1]
    teacher_partial = jnp.dot(
        lax.all_gather(teacher_in, "tp", axis=0, tiled=True),
        teacher_pair,
        preferred_element_type=fl,
    )
    teacher_pre = lax.psum_scatter(teacher_partial, "grp", scatter_dimension=0, tiled=True)
    teacher_hidden = (
        jax.nn.silu(teacher_pre[:, :teacher_width]) * teacher_pre[:, teacher_width:]
    ).astype(bf)
    teacher_sums = jnp.dot(
        lax.all_gather(teacher_hidden, "grp", axis=0, tiled=True),
        teacher_down,
        preferred_element_type=fl,
    )
    teacher_share = lax.psum_scatter(teacher_sums, "tp", scatter_dimension=1, tiled=True)
    teacher_feature = lax.all_to_all(
        teacher_share.astype(bf), "grp", split_axis=0, concat_axis=1, tiled=True
    )
    student_pair = jnp.concatenate([student_gate, student_up], axis=1)
    student_width = student_gate.shape[1]
    input_rows = lax.all_gather(student_in, "tp", axis=0, tiled=True)
    student_partial = jnp.dot(input_rows, student_pair, preferred_element_type=fl)
    student_pre = lax.psum_scatter(student_partial, "grp", scatter_dimension=0, tiled=True)
    gate_values = student_pre[:, :student_width]
    up_values = student_pre[:, student_width:]
    student_hidden = (jax.nn.silu(gate_values) * up_values).astype(bf)
    hidden_rows = lax.all_gather(student_hidden, "grp", axis=0, tiled=True)
    feature_sum = lax.psum(jnp.dot(hidden_rows, student_down, preferred_element_type=fl), "tp")
    student_feature = feature_sum.astype(bf)
    proj_matrix = projector.reshape(projector.shape[0], -1)
    projected = lax.psum_scatter(
        jnp.dot(student_feature, proj_matrix, preferred_element_type=fl),
        "grp",
        scatter_dimension=0,
        tiled=True,
    )
    residual_grad = (projected - teacher_feature.astype(fl)).astype(bf)
    residual_rows = lax.all_gather(residual_grad, "grp", axis=0, tiled=True)
    grad_projector = jnp.dot(student_feature.T, residual_rows, preferred_element_type=fl).reshape(
        projector.shape
    )
    feature_grad = lax.psum(
        jnp.dot(residual_rows, proj_matrix.T, preferred_element_type=fl), "tp"
    ).astype(bf)
    grad_down = jnp.dot(hidden_rows.T, feature_grad, preferred_element_type=fl)
    hidden_grad = lax.psum_scatter(
        jnp.dot(feature_grad, student_down.T, preferred_element_type=fl),
        "grp",
        scatter_dimension=0,
        tiled=True,
    )
    sigmoid_gate = jax.nn.sigmoid(gate_values)
    gate_grad = (
        hidden_grad * up_values * sigmoid_gate * (1.0 + gate_values * (1.0 - sigmoid_gate))
    ).astype(bf)
    up_grad = (hidden_grad * gate_values * sigmoid_gate).astype(bf)
    pair_rows = lax.all_gather(
        jnp.concatenate([gate_grad, up_grad], axis=1), "grp", axis=0, tiled=True
    )
    grad_pair = jnp.dot(input_rows.T, pair_rows, preferred_element_type=fl)
    grad_input = lax.psum_scatter(
        jnp.dot(pair_rows, student_pair.T, preferred_element_type=fl).astype(jnp.bfloat16),
        "tp",
        scatter_dimension=0,
        tiled=True,
    ).astype(jnp.float32)
    return (
        grad_input,
        grad_pair[:, :student_width],
        grad_pair[:, student_width:],
        grad_down,
        grad_projector,
    )


def solution(mesh):
    placed = (
        P("tp", "grp"),
        P("grp", "tp"),
        P("grp", "tp"),
        P("tp", "grp"),
        P("tp", "grp"),
        P("grp", "tp"),
        P("grp", "tp"),
        P("tp", "grp"),
        P("grp", None, "tp"),
    )
    return jax.shard_map(
        body,
        mesh=mesh,
        in_specs=placed,
        out_specs=(
            P("tp", "grp"),
            P("grp", "tp"),
            P("grp", "tp"),
            P("tp", "grp"),
            P("grp", None, "tp"),
        ),
        check_vma=False,
    )
```

profile of v0, /device:TPU:0, one launch (start us, length us, event | category | flops | bytes accessed | tf_op | source)
XLA Modules:
  0.0 422.7 jit_solution(930207206825908747)
XLA Ops:
  7.2 0.0 reduce-scatter.11.cloned.1.call-start
  7.2 17.4 %all_gather.20 = bf16[192,2048]{1,0:T(8,128)(2,1)S(1)} all-gather(bf16[24,2048]{1,0:T(8,128)(2,1)} %param.9), channel_id=1, replica_groups=mesh['grp'=4,'tp'=8] {'tp'}, dimensions={0}, use_global_device_ids=true | all-gather | bytes 884736 | tf_op jit(solution)/shard_map/all_gather | solution.py:23
  24.6 14.3 %fusion.4 = f32[192,7168]{1,0:T(8,128)} fusion(bf16[192,2048]{1,0:T(8,128)(2,1)S(1)} %all_gather.20, bf16[2048,3584]{1,0:T(8,128)(2,1)} %param.11, bf16[2048,3584]{1,0:T(8,128)(2,1)} %param.10), kind=kOutput, calls=%fused_computation.4 | convolution fusion | flops 5695864832 | bytes 35651584 | tf_op jit(solution)/shard_map/dot_general | solution.py:22
  39.0 0.0 all-gather.3.cloned.1.call-start
  39.0 64.8 %reduce-scatter.11.cloned.1.call-done = f32[48,7168]{1,0:T(8,128)} async-done(((f32[192,7168]{1,0:T(8,128)}), f32[48,7168]{1,0:T(8,128)}) %reduce-scatter.11.cloned.1.call-update) | async-done | bytes 1376272 | tf_op jit(solution)/shard_map/reduce_scatter | solution.py:27
  103.8 2.2 fusion.7
  106.0 0.0 reduce-scatter.7.cloned.1.call-start
  106.1 14.6 %all_gather.18 = bf16[192,1024]{1,0:T(8,128)(2,1)S(1)} all-gather(bf16[24,1024]{1,0:T(8,128)(2,1)S(1)} %copy-done.8), channel_id=1, replica_groups=mesh['grp'=4,'tp'=8] {'tp'}, dimensions={0}, use_global_device_ids=true | all-gather | bytes 442368 | tf_op jit(solution)/shard_map/all_gather | solution.py:42
  120.7 2.5 constant_dynamic-update-slice_fusion.1
  123.2 0.3 constant_dynamic-update-slice_fusion
  123.5 3.0 copy-done
  126.6 3.1 convolution_bitcast_fusion.1
  129.7 0.0 reduce-scatter.13.cloned.1.call-start
  129.8 5.7 %all-gather.3.cloned.1.call-done = bf16[192,3584]{1,0:T(8,128)(2,1)} async-done(((bf16[48,3584]{1,0:T(8,128)(2,1)}), bf16[192,3584]{1,0:T(8,128)(2,1)}) %all-gather.3.cloned.1.call-update) | async-done | bytes 1376272 | tf_op jit(solution)/shard_map/all_gather | solution.py:32
  135.4 9.8 %fusion.19 = f32[192,2048]{1,0:T(8,128)} fusion(bf16[192,3584]{1,0:T(8,128)(2,1)} %all-gather.3.cloned.1.call-done, bf16[3584,2048]{1,0:T(8,128)(2,1)} %param.12), kind=kOutput, calls=%fused_computation.30 | convolution fusion | flops 2818572288 | bytes 17629184 | tf_op jit(solution)/shard_map/dot_general | solution.py:31
  145.2 0.0 reduce-scatter.9.cloned.1.call-start
  145.3 2.2 copy.23
  147.4 32.3 %reduce-scatter.7.cloned.1.call-done = f32[48,3584]{1,0:T(8,128)} async-done(((f32[192,3584]{1,0:T(8,128)}), f32[48,3584]{1,0:T(8,128)}) %reduce-scatter.7.cloned.1.call-update) | async-done | bytes 688144 | tf_op jit(solution)/shard_map/reduce_scatter | solution.py:44
  179.7 1.2 multiply_convert_fusion.2
  180.9 10.7 %all_gather.19 = bf16[192,1792]{1,0:T(8,128)(2,1)S(1)} all-gather(bf16[48,1792]{1,0:T(8,128)(2,1)S(1)} %multiply_convert_fusion.2), channel_id=1, replica_groups=mesh['grp'=4,'tp'=8] {'grp'}, dimensions={0}, use_global_device_ids=true | all-gather | bytes 860160 | tf_op jit(solution)/shard_map/all_gather | solution.py:48
  191.6 3.8 fusion.18
  195.4 38.1 %all-reduce.2 = bf16[192,1024]{1,0:T(8,128)(2,1)S(1)} all-reduce(f32[192,1024]{1,0:T(8,128)} %fusion.18), channel_id=1, replica_groups=mesh['grp'=4,'tp'=8] {'tp'}, use_global_device_ids=true, to_apply=%region_1.2 | all-reduce | flops 196608 | bytes 1179648 | tf_op jit(solution)/shard_map/psum | solution.py:49
  233.5 1.5 fusion.24
  235.0 0.0 reduce-scatter.15.cloned.1.call-start
  235.1 0.9 convert_element_type.42
  236.1 7.8 %all_to_all.13 = bf16[4,48,256]{2,1,0:T(8,128)(2,1)S(1)} all-to-all(bf16[4,48,256]{2,1,0:T(8,128)(2,1)S(1)} %bitcast.40), channel_id=1, replica_groups=mesh['grp'=4,'tp'=8] {'grp'}, dimensions={0} | all-to-all | bytes 196608 | tf_op jit(solution)/shard_map/all_to_all | solution.py:37
  243.9 14.5 %reduce-scatter.9.cloned.1.call-done = f32[48,1024]{1,0:T(8,128)} async-done(((f32[192,1024]{1,0:T(8,128)}), f32[48,1024]{1,0:T(8,128)}) %reduce-scatter.9.cloned.1.call-update) | async-done | bytes 196624 | tf_op jit(solution)/shard_map/reduce_scatter | solution.py:52
  258.4 0.9 subtract_convert_fusion
  259.4 9.6 %all_gather.22 = bf16[192,1024]{1,0:T(8,128)(2,1)S(1)} all-gather(bf16[48,1024]{1,0:T(8,128)(2,1)S(1)} %subtract_convert_fusion), channel_id=1, replica_groups=mesh['grp'=4,'tp'=8] {'grp'}, dimensions={0}, use_global_device_ids=true | all-gather | bytes 491520 | tf_op jit(solution)/shard_map/all_gather | solution.py:59
  268.9 0.7 copy-done.4
  269.7 1.7 fusion.20
  271.4 35.0 %all-reduce.3 = bf16[192,1024]{1,0:T(8,128)(2,1)S(1)} all-reduce(f32[192,1024]{1,0:T(8,128)} %fusion.20), channel_id=1, replica_groups=mesh['grp'=4,'tp'=8] {'tp'}, use_global_device_ids=true, to_apply=%region_5.6 | all-reduce | flops 196608 | bytes 1179648 | tf_op jit(solution)/shard_map/psum | solution.py:63
  306.4 4.5 %fusion.22 = f32[192,1792]{1,0:T(8,128)} fusion(bf16[192,1024]{1,0:T(8,128)(2,1)S(1)} %all-reduce.3, bf16[1792,1024]{1,0:T(8,128)(2,1)} %param.16), kind=kOutput, calls=%fused_computation.33 | convolution fusion | flops 704643072 | bytes 5439488 | tf_op jit(solution)/shard_map/dot_general | solution.py:68
  310.9 0.2 all-gather.5.cloned.1.call-start
  311.1 27.0 %reduce-scatter.15.cloned.1.call-done = f32[48,1792]{1,0:T(8,128)} async-done(((f32[192,1792]{1,0:T(8,128)}), f32[48,1792]{1,0:T(8,128)}) %reduce-scatter.15.cloned.1.call-update) | async-done | bytes 344080 | tf_op jit(solution)/shard_map/reduce_scatter | solution.py:67
  338.2 1.1 multiply_convert_fusion.1
  339.3 0.7 pad_maximum_fusion
  340.1 0.0 reduce-scatter.17.cloned.1.call-start
  340.1 2.8 fusion.23
  342.9 5.3 %copy.21 = f32[1024,4,256]{2,1,0:T(4,128)} copy(f32[1024,4,256]{0,2,1:T(8,128)} %bitcast.35) | data formatting | bytes 8388608
  348.2 4.2 fusion.21
  352.4 17.1 %all-gather.5.cloned.1.call-done = bf16[192,3584]{1,0:T(8,128)(2,1)} async-done(((bf16[48,3584]{1,0:T(8,128)(2,1)}), bf16[192,3584]{1,0:T(8,128)(2,1)}) %all-gather.5.cloned.1.call-update) | async-done | bytes 1376272 | tf_op jit(solution)/shard_map/all_gather | solution.py:78
  369.4 6.9 %convolution_convert_fusion = bf16[192,1024]{1,0:T(8,128)(2,1)} fusion(bf16[192,3584]{1,0:T(8,128)(2,1)} %all-gather.5.cloned.1.call-done, bf16[1024,3584]{1,0:T(8,128)(2,1)} %copy-done), kind=kOutput, calls=%fused_computation.7 | convolution fusion | flops 1409482752 | bytes 9109504 | tf_op jit(solution)/shard_map/dot_general | solution.py:83
  376.4 7.3 %convolution_bitcast_fusion = f32[1024,3584]{0,1:T(8,128)} fusion(bf16[192,3584]{1,0:T(8,128)(2,1)S(1)} %copy-done.7, bf16[192,1024]{1,0:T(8,128)(2,1)S(1)} %copy-done.2), kind=kOutput, calls=%fused_computation.5 | convolution fusion | flops 1409286144 | bytes 16449536 | tf_op jit(solution)/shard_map/dot_general | solution.py:81
  383.7 13.9 %fusion.17 = (f32[1024,1792]{0,1:T(8,128)}, f32[1024,1792]{0,1:T(8,128)}) fusion(f32[1024,3584]{0,1:T(8,128)} %convolution_bitcast_fusion), kind=kLoop, calls=%fused_computation.28 | loop fusion | bytes 29360128 | tf_op jit(solution)/shard_map/slice | solution.py:91
  397.6 8.4 %copy.19 = f32[1024,1792]{1,0:T(8,128)} copy(f32[1024,1792]{0,1:T(8,128)} %get-tuple-element.16) | data formatting | bytes 14680064
  406.0 8.4 %copy.20 = f32[1024,1792]{1,0:T(8,128)} copy(f32[1024,1792]{0,1:T(8,128)} %get-tuple-element.15) | data formatting | bytes 14680064
  414.4 1.4 convert_element_type.51
  (28 shorter events, 0.2 us)
Async XLA Ops:
  7.2 96.6 %reduce-scatter.11.cloned.1.call-start = ((), (), s32[]{:S(2)}) async-start(), calls=%async_computation.9 | async-start | bytes 6881280 | tf_op jit(solution)/shard_map/reduce_scatter | solution.py:27
  38.9 67.1 %copy-start.8 = (bf16[24,1024]{1,0:T(8,128)(2,1)S(1)}, bf16[24,1024]{1,0:T(8,128)(2,1)}, u32[]{:S(2)}) copy-start(bf16[24,1024]{1,0:T(8,128)(2,1)} %param.13) | copy-start | bytes 147460
  39.0 96.5 %all-gather.3.cloned.1.call-start = ((), (), s32[]{:S(2)}) async-start(), calls=%async_computation.10 | async-start | bytes 1720320 | tf_op jit(solution)/shard_map/all_gather | solution.py:32
  106.0 73.7 %reduce-scatter.7.cloned.1.call-start = ((), (), s32[]{:S(2)}) async-start(), calls=%async_computation.7 | async-start | bytes 3440640 | tf_op jit(solution)/shard_map/reduce_scatter | solution.py:44
  106.1 17.1 %copy-start.3 = (bf16[1024,1792]{1,0:T(8,128)(2,1)S(1)}, bf16[1024,1792]{1,0:T(8,128)(2,1)}, u32[]{:S(2)}) copy-start(bf16[1024,1792]{1,0:T(8,128)(2,1)} %param.15) | copy-start | bytes 11010052
  120.7 2.8 copy-start.1
  123.5 3.1 copy-start
  129.7 105.4 %reduce-scatter.13.cloned.1.call-start = ((), (), s32[]{:S(2)}) async-start(), calls=%async_computation.11 | async-start | bytes 1769472 | tf_op jit(solution)/shard_map/reduce_scatter | solution.py:36
  145.2 113.2 %reduce-scatter.9.cloned.1.call-start = ((), (), s32[]{:S(2)}) async-start(), calls=%async_computation.8 | async-start | bytes 983040 | tf_op jit(solution)/shard_map/reduce_scatter | solution.py:52
  235.0 103.1 %reduce-scatter.15.cloned.1.call-start = ((), (), s32[]{:S(2)}) async-start(), calls=%async_computation.12 | async-start | bytes 1720320 | tf_op jit(solution)/shard_map/reduce_scatter | solution.py:67
  268.9 0.7 copy-start.4
  271.4 66.8 %copy-start.6 = (f32[48,3584]{1,0:T(8,128)S(1)}, f32[48,3584]{1,0:T(8,128)}, u32[]{:S(2)}) copy-start(f32[48,3584]{1,0:T(8,128)} %reduce-scatter.7.cloned.1.call-done) | copy-start | bytes 2064388
  271.4 68.7 %copy-start.5 = (bf16[192,1024]{1,0:T(8,128)(2,1)S(1)}, bf16[192,1024]{1,0:T(8,128)(2,1)}, u32[]{:S(2)}) copy-start(bf16[192,1024]{1,0:T(8,128)(2,1)} %copy-done.4) | copy-start | bytes 1179652
  310.9 58.5 %all-gather.5.cloned.1.call-start = ((), (), s32[]{:S(2)}) async-start(), calls=%async_computation.13 | async-start | bytes 1720320 | tf_op jit(solution)/shard_map/all_gather | solution.py:78
  340.1 74.3 %reduce-scatter.17.cloned.1.call-start = ((), (), s32[]{:S(2)}) async-start(), calls=%async_computation.14 | async-start | bytes 442368 | tf_op jit(solution)/shard_map/reduce_scatter | solution.py:82
  352.4 24.0 %copy-start.2 = (bf16[192,1024]{1,0:T(8,128)(2,1)S(1)}, bf16[192,1024]{1,0:T(8,128)(2,1)}, u32[]{:S(2)}) copy-start(bf16[192,1024]{1,0:T(8,128)(2,1)} %copy-done.1) | copy-start | bytes 1179652
  369.4 6.9 %copy-start.7 = (bf16[192,3584]{1,0:T(8,128)(2,1)S(1)}, bf16[192,3584]{1,0:T(8,128)(2,1)}, u32[]{:S(2)}) copy-start(bf16[192,3584]{1,0:T(8,128)(2,1)} %all-gather.5.cloned.1.call-done) | copy-start | bytes 4128772
Sparse Core Ops, SparseCore 0:
  39.1 64.6 reduce-scatter.10
  106.2 29.1 all-gather.2
  139.0 40.6 reduce-scatter.6
  182.4 36.0 reduce-scatter.12
  235.2 23.2 reduce-scatter.8
  311.0 27.0 reduce-scatter.14
  340.2 29.1 all-gather.4
  376.5 31.1 reduce-scatter.16
where the time goes:
time: 424 us; the launch traced here: 423 us
  waiting for transfers between devices  161 us (38%)
  blocking collectives  133 us (31%)
  matrix products  59.9 us (14%)
  local copies, waits for them, and re-layouts  44.7 us (11%)
  between operations  14.3 us (3%)
  other arithmetic  8.64 us (2%)
    reduce_scatter x1, waiting for transfers between devices, body(): lax.psum_scatter(teacher_partial, 'grp', scatter_dimension=0, tiled=True)  64.8 us
    psum x1, blocking collectives, body(): lax.psum(jnp.dot(hidden_rows, student_down, preferred_element_type=fl), '...  38.1 us
    psum x1, blocking collectives, body(): lax.psum(jnp.dot(residual_rows, proj_matrix.T, preferred_element_type=fl)...  35 us
    reduce_scatter x1, waiting for transfers between devices, body(): lax.psum_scatter(student_partial, 'grp', scatter_dimension=0, tiled=True)  32.3 us
    unnamed x23, local copies, waits for them, and re-layouts  30.4 us
    reduce_scatter x1, waiting for transfers between devices, body(): lax.psum_scatter(jnp.dot(feature_grad, student_down.T, preferred_element_...  27 us
    all_gather x1, blocking collectives, body(): lax.all_gather(teacher_in, 'tp', axis=0, tiled=True)  17.4 us
    all_gather x1, waiting for transfers between devices, body(): lax.all_gather(jnp.concatenate([gate_grad, up_grad], axis=1), 'grp', axis...  17.1 us
  transfers between devices with their start and end apart: 8, of which 6 were waited for; matrix products, arithmetic and copies ran while one was open for 18% of the time, Pallas kernels for 0%

commit v1 on v0

v1 whole, which is shorter than its diff:
```python
import jax
import jax.numpy as jnp
from jax import lax
from jax.sharding import PartitionSpec as P

BF = jnp.bfloat16
FL = jnp.float32


def swap(x, axis, size, k):
    return lax.ppermute(x, axis, [(i, i ^ k) for i in range(size)])


def dot(a, b):
    return jnp.dot(a, b, preferred_element_type=FL)


def dot_t(a, b):
    return lax.dot_general(a, b, (((1,), (1,)), ((), ())), preferred_element_type=FL)


def t_dot(a, b):
    return lax.dot_general(a, b, (((0,), (0,)), ((), ())), preferred_element_type=FL)


def make_body(n_grp, n_tp):
    def grp(x, k):
        return swap(x, "grp", n_grp, k)

    def tp(x, k):
        return swap(x, "tp", n_tp, k)

    def tp_pieces(x):
        even = {0: x}
        for k in range(2, n_tp, 2):
            even[k] = tp(x, k)
        out = []
        for k in range(0, n_tp, 2):
            out += [even[k], tp(even[k], 1)]
        return out

    def grp_scatter(parts):
        total = parts[0].astype(FL)
        for k in range(1, n_grp):
            total = total + grp(parts[k].astype(BF), k).astype(FL)
        return total

    def grp_gather(own):
        return [own] + [grp(own, k) for k in range(1, n_grp)]

    def tp_sum(y, core):
        half = y.shape[1] // 2
        y = y.astype(BF)
        left, right = y[:, :half], y[:, half:]
        mine = jnp.where(core == 0, left, right)
        other = jnp.where(core == 0, right, left)
        total = mine.astype(FL) + tp(other, 1).astype(FL)
        k = 2
        while k < n_tp:
            total = total.astype(BF)
            total = total.astype(FL) + tp(total, k).astype(FL)
            k *= 2
        total = total.astype(BF)
        other = tp(total, 1)
        return jnp.where(
            core == 0,
            jnp.concatenate([total, other], axis=1),
            jnp.concatenate([other, total], axis=1),
        )

    def body(
        teacher_in,
        teacher_gate,
        teacher_up,
        teacher_down,
        student_in,
        student_gate,
        student_up,
        student_down,
        projector,
    ):
        g = lax.axis_index("grp")
        t = lax.axis_index("tp")
        core = t % 2
        share = student_in.shape[0]
        tokens = share * n_tp
        rows = tokens // n_grp

        order = lax.broadcasted_iota(jnp.int32, (tokens, tokens), 0)
        token = ((order // rows) ^ g) * rows + order % rows
        source = ((token // share) ^ t) * share + token % share
        pick = (source == lax.broadcasted_iota(jnp.int32, (tokens, tokens), 1)).astype(BF)

        def local_rows(x):
            return dot(pick, jnp.concatenate(tp_pieces(x), axis=0)).astype(BF)

        def chunks(y):
            return [y[k * rows : (k + 1) * rows] for k in range(n_grp)]

        student_rows = local_rows(student_in)
        teacher_rows = local_rows(teacher_in)

        gate_values = grp_scatter(chunks(dot(student_rows, student_gate).astype(BF)))
        up_values = grp_scatter(chunks(dot(student_rows, student_up).astype(BF)))
        sigmoid_gate = jax.nn.sigmoid(gate_values)
        student_hidden = (gate_values * sigmoid_gate * up_values).astype(BF)
        hidden_rows = jnp.concatenate(grp_gather(student_hidden), axis=0)
        student_feature = tp_sum(dot(hidden_rows, student_down), core)

        width = teacher_gate.shape[1]
        pieces = 2
        step = width // pieces
        teacher_sums = 0.0
        for p in range(pieces):
            cut = slice(p * step, (p + 1) * step)
            pre = grp_scatter(chunks(dot(teacher_rows, teacher_gate[:, cut]).astype(BF)))
            lin = grp_scatter(chunks(dot(teacher_rows, teacher_up[:, cut]).astype(BF)))
            teacher_hidden = (jax.nn.silu(pre) * lin).astype(BF)
            teacher_hidden = jnp.concatenate(grp_gather(teacher_hidden), axis=0)
            teacher_sums = teacher_sums + dot(teacher_hidden, teacher_down[cut])
        teacher_sums = teacher_sums.astype(BF)
        cols = teacher_sums.shape[1] // n_tp

        def teacher_cols(k):
            return lax.dynamic_slice_in_dim(teacher_sums, (t ^ k) * cols, cols, axis=1)

        teacher_share = 0.0
        for k in range(0, n_tp, 2):
            both = teacher_cols(k).astype(FL) + tp(teacher_cols(k + 1), 1).astype(FL)
            if k:
                both = tp(both.astype(BF), k).astype(FL)
            teacher_share = teacher_share + both
        teacher_share = teacher_share.astype(BF).astype(FL)

        proj_blocks = [
            lax.dynamic_index_in_dim(projector, g ^ k, axis=1, keepdims=False)
            for k in range(n_grp)
        ]
        proj_local = jnp.concatenate(proj_blocks, axis=1)
        block = projector.shape[2]

        def from_peer(x, k):
            return jnp.concatenate([x[(k ^ m) * rows : ((k ^ m) + 1) * rows] for m in range(n_grp)])

        projected = dot(student_feature, proj_local)
        residual = projected[:, :block] - teacher_share
        for k in range(1, n_grp):
            got = grp(projected[:, k * block : (k + 1) * block].astype(BF), k)
            residual = residual + from_peer(got, k).astype(FL)
        residual = residual.astype(BF)
        got = grp_gather(residual)
        residual_rows = jnp.concatenate(
            [from_peer(got[k], k) if k else got[k] for k in range(n_grp)], axis=1
        )
        feature_grad = tp_sum(dot_t(residual_rows, proj_local), core)

        ordered = [
            lax.dynamic_index_in_dim(
                residual_rows.reshape(tokens, n_grp, block), g ^ k, axis=1, keepdims=False
            )
            for k in range(n_grp)
        ]
        grad_projector = t_dot(student_feature, jnp.concatenate(ordered, axis=1)).reshape(
            projector.shape
        )
        grad_down = t_dot(hidden_rows, feature_grad)

        gate_factor = (
            up_values * sigmoid_gate * (1.0 + gate_values * (1.0 - sigmoid_gate))
        ).astype(BF)
        up_factor = (gate_values * sigmoid_gate).astype(BF)
        gate_factor = grp_gather(gate_factor)
        up_factor = grp_gather(up_factor)

        hidden_grad = grp_scatter(chunks(dot_t(feature_grad, student_down).astype(BF))).astype(BF)
        hidden_grad = grp_gather(hidden_grad)
        gate_grad = jnp.concatenate(
            [(h.astype(FL) * f.astype(FL)).astype(BF) for h, f in zip(hidden_grad, gate_factor)]
        )
        up_grad = jnp.concatenate(
            [(h.astype(FL) * f.astype(FL)).astype(BF) for h, f in zip(hidden_grad, up_factor)]
        )
        input_sums = (dot_t(gate_grad, student_gate) + dot_t(up_grad, student_up)).astype(BF)
        pitch = -(-share // 16) * 16
        slot = lax.broadcasted_iota(jnp.int32, (pitch * n_tp, tokens), 0)
        wanted = ((slot // pitch) ^ t) * share + slot % pitch
        place = ((wanted // rows) ^ g) * rows + wanted % rows
        column = lax.broadcasted_iota(jnp.int32, (pitch * n_tp, tokens), 1)
        send = dot(((place == column) & (slot % pitch < share)).astype(BF), input_sums).astype(BF)

        def piece(k):
            return send[k * pitch : k * pitch + share]

        grad_input = 0.0
        for k in range(0, n_tp, 2):
            both = piece(k).astype(FL) + tp(piece(k + 1), 1).astype(FL)
            if k:
                both = tp(both.astype(BF), k).astype(FL)
            grad_input = grad_input + both

        grad_gate = t_dot(student_rows, gate_grad)
        grad_up = t_dot(student_rows, up_grad)
        return grad_input, grad_gate, grad_up, grad_down, grad_projector

    return body


def solution(mesh):
    placed = (
        P("tp", "grp"),
        P("grp", "tp"),
        P("grp", "tp"),
        P("tp", "grp"),
        P("tp", "grp"),
        P("grp", "tp"),
        P("grp", "tp"),
        P("tp", "grp"),
        P("grp", None, "tp"),
    )
    return jax.shard_map(
        make_body(mesh.shape["grp"], mesh.shape["tp"]),
        mesh=mesh,
        in_specs=placed,
        out_specs=(
            P("tp", "grp"),
            P("grp", "tp"),
            P("grp", "tp"),
            P("tp", "grp"),
            P("grp", None, "tp"),
        ),
        check_vma=False,
    )
```

time: 424 us -> 237 us (0.56)
  blocking collectives: 133 us -> 0 us
  waiting for transfers between devices: 161 us -> 75 us
  starting transfers between devices: 0.51 us -> 77.5 us
  local copies, waits for them, and re-layouts: 44.7 us -> 28.3 us
  between operations: 14.3 us -> 1.62 us
  matrix products: 59.9 us -> 49.8 us
    reduce_scatter x6 -> x0, waiting for transfers between devices: 139 us -> none  [the longest x1 64.8 us: body(): lax.psum_scatter(teacher_partial, 'grp', scatter_dimension=0, tiled=True)]
    ppermute x0 -> x81, starting transfers between devices: none -> 77.5 us  [swap(): return lax.ppermute(x, axis, [(i, i ^ k) for i in range(size)])]
    ppermute x0 -> x81, waiting for transfers between devices: none -> 75 us  [swap(): return lax.ppermute(x, axis, [(i, i ^ k) for i in range(size)])]
    psum x2 -> x0, blocking collectives: 73.1 us -> none  [the longest x1 38.1 us: body(): lax.psum(jnp.dot(hidden_rows, student_down, preferred_element_type=fl), '...]
    all_gather x4 -> x0, blocking collectives: 52.4 us -> none  [the longest x1 17.4 us: body(): lax.all_gather(teacher_in, 'tp', axis=0, tiled=True)]
    all_gather x2 -> x0, waiting for transfers between devices: 22.7 us -> none  [the longest x1 17.1 us: body(): lax.all_gather(jnp.concatenate([gate_grad, up_grad], axis=1), 'grp', axis...]
    unnamed x23 -> x89, local copies, waits for them, and re-layouts: 30.4 us -> 15.7 us
    slice x1 -> x15, local copies, waits for them, and re-layouts: 13.9 us -> 1.12 us  [the longest x7 1.04 us: chunks(): return [y[k * rows:(k + 1) * rows] for k in range(n_grp)]]
  transfers between devices with their start and end apart: 8 -> 81, of which waited for: 6 -> 29; matrix products, arithmetic and copies ran while one was open for 18% -> 29% of each run, Pallas kernels for 0% -> 0%
where the time goes in v1:
time: 237 us
  starting transfers between devices  77.5 us (33%)
  waiting for transfers between devices  75 us (32%)
  matrix products  49.8 us (21%)
  local copies, waits for them, and re-layouts  28.3 us (12%)
  other arithmetic  4.55 us (2%)
    ppermute x81, starting transfers between devices, swap(): return lax.ppermute(x, axis, [(i, i ^ k) for i in range(size)])  77.5 us
    ppermute x81, waiting for transfers between devices, swap(): return lax.ppermute(x, axis, [(i, i ^ k) for i in range(size)])  75 us
    dot_general x13, matrix products, dot(): return jnp.dot(a, b, preferred_element_type=FL)  27.4 us
    dot_general x4, matrix products, t_dot(): lax.dot_general(a, b, (((0,), (0,)), ((), ())), preferred_element_type=FL)  16.6 us
    unnamed x89, local copies, waits for them, and re-layouts  15.7 us
    dynamic_slice x1, local copies, waits for them, and re-layouts, body(): lax.dynamic_index_in_dim(projector, g ^ k, axis=1, keepdims=False)  8.37 us
    dot_general x3, matrix products, dot_t(): lax.dot_general(a, b, (((1,), (1,)), ((), ())), preferred_element_type=FL)  5.79 us
  transfers between devices with their start and end apart: 81, of which 29 were waited for; matrix products, arithmetic and copies ran while one was open for 29% of the time, Pallas kernels for 0%

profile of v1, /device:TPU:0, one launch (start us, length us, event | category | flops | bytes accessed | tf_op | source)
XLA Modules:
  0.0 236.8 jit_solution(13461367539009756612)
XLA Ops:
  0.6 4.1 %collective-permute-start.3 = (bf16[24,1024]{1,0:T(8,128)(2,1)}, bf16[24,1024]{1,0:T(8,128)(2,1)}, u32[]{:S(2)}, u32[]{:S(2)}) collective-permute-start(bf16[24,1024]{1,0:T(8,128)(2,1)} %param.13), channel_id=1, source_target_pairs={{0,4},{1,5},{2,6},{3,7},{4,0},{5,1},{6,2},{7,3},{8,12},{9,13},{10,... | collective-permute-start | bytes 147464 | tf_op jit(solution)/shard_map/ppermute | solution.py:11
  4.8 1.6 collective-permute-start.1
  6.3 1.9 collective-permute-start.23
  9.7 1.5 constant_dynamic-update-slice_fusion.15
  11.2 8.4 %constant_dynamic-slice_fusion.11 = (bf16[1024,1,256]{2,1,0:T(2,128)(2,1)S(1)}, bf16[1024,1,256]{2,1,0:T(2,128)(2,1)S(1)}, bf16[1024,1,256]{2,1,0:T(2,128)(2,1)S(1)}, bf16[1024,1,256]{2,1,0:T(2,128)(2,1)S(1)}) fusion(bf16[1024,4,256]{2,1,0:T(4,128)(2,1)} %param.17, s32[]{:T(128)S(6)} %select_n.135, s32[]{:T(128)S(6)} %select_n.137, s32[]{:T(128)S(6)} %select_n.136, ...), kind=kLoop, calls=%fused_computation.184 | loop fusion | bytes 4194320 | tf_op jit(solution)/shard_map/jit(dynamic_index_in_dim)/dynamic_slice | solution.py:136
  21.0 2.5 %collective-permute-start.21 = (bf16[24,2048]{1,0:T(8,128)(2,1)S(1)}, bf16[24,2048]{1,0:T(8,128)(2,1)S(1)}, u32[]{:S(2)}, u32[]{:S(2)}) collective-permute-start(bf16[24,2048]{1,0:T(8,128)(2,1)S(1)} %copy-done.21), channel_id=1, source_target_pairs={{0,2},{1,3},{2,0},{3,1},{4,6},{5,7},{6,4},{7,5},{8,10},{9,11},{10,... | collective-permute-start | bytes 294920 | tf_op jit(solution)/shard_map/ppermute | solution.py:11
  32.1 3.1 %convolution_convert_fusion.3 = bf16[192,1792]{1,0:T(8,128)(2,1)S(1)} fusion(bf16[192,1024]{1,0:T(8,128)(2,1)S(1)} %convolution_convert_fusion.7, bf16[1024,1792]{1,0:T(8,128)(2,1)} %param.14), kind=kOutput, calls=%fused_computation.21 | convolution fusion | flops 704987136 | bytes 4751360 | tf_op jit(solution)/shard_map/dot_general | solution.py:15
  35.2 1.6 collective-permute-start.7
  37.7 1.6 collective-permute-start.9
  40.8 1.6 collective-permute-start.10
  45.5 4.9 %fusion.27 = bf16[192,1792]{1,0:T(8,128)(2,1)S(1)} fusion(bf16[192,2048]{1,0:T(8,128)(2,1)S(1)} %convolution_convert_fusion.1, bf16[2048,3584]{1,0:T(8,128)(2,1)} %param.11), kind=kOutput, calls=%fused_computation.17 | convolution fusion | flops 1409630208 | bytes 8814592 | tf_op jit(solution)/shard_map/dot_general | solution.py:15
  50.5 1.8 copy-done.23
  52.2 1.6 fusion.21
  53.8 4.9 %fusion.24 = bf16[192,1792]{1,0:T(8,128)(2,1)S(1)} fusion(bf16[192,2048]{1,0:T(8,128)(2,1)S(1)} %convolution_convert_fusion.1, bf16[2048,3584]{1,0:T(8,128)(2,1)} %param.10), kind=kOutput, calls=%fused_computation.16 | convolution fusion | flops 1409630208 | bytes 8814592 | tf_op jit(solution)/shard_map/dot_general | solution.py:15
  58.8 1.6 fusion.18
  64.2 2.6 %collective-permute-done.11 = bf16[48,1792]{1,0:T(8,128)(2,1)S(1)} collective-permute-done((bf16[48,1792]{1,0:T(8,128)(2,1)S(1)}, bf16[48,1792]{1,0:T(8,128)(2,1)S(1)}, u32[]{:S(2)}, u32[]{:S(2)}) %collective-permute-start.11) | collective-permute-done | bytes 172064 | tf_op jit(solution)/shard_map/ppermute | solution.py:11
  67.1 1.7 collective-permute-start.15
  70.7 6.2 %collective-permute-done.15 = bf16[48,1792]{1,0:T(8,128)(2,1)S(1)} collective-permute-done((bf16[48,1792]{1,0:T(8,128)(2,1)S(1)}, bf16[48,1792]{1,0:T(8,128)(2,1)S(1)}, u32[]{:S(2)}, u32[]{:S(2)}) %collective-permute-start.15) | collective-permute-done | bytes 172064 | tf_op jit(solution)/shard_map/ppermute | solution.py:11
  80.2 1.7 collective-permute-start.38
  85.0 1.6 collective-permute-start.29
  87.6 3.2 %collective-permute-done.38 = bf16[48,1792]{1,0:T(8,128)(2,1)S(1)} collective-permute-done((bf16[48,1792]{1,0:T(8,128)(2,1)S(1)}, bf16[48,1792]{1,0:T(8,128)(2,1)S(1)}, u32[]{:S(2)}, u32[]{:S(2)}) %collective-permute-start.38) | collective-permute-done | bytes 172064 | tf_op jit(solution)/shard_map/ppermute | solution.py:11
  91.8 2.1 collective-permute-done.37
  99.5 1.7 collective-permute-done.28
  103.1 2.6 %collective-permute-done.32 = bf16[48,1792]{1,0:T(8,128)(2,1)S(1)} collective-permute-done((bf16[48,1792]{1,0:T(8,128)(2,1)S(1)}, bf16[48,1792]{1,0:T(8,128)(2,1)S(1)}, u32[]{:S(2)}, u32[]{:S(2)}) %collective-permute-start.32) | collective-permute-done | bytes 172064 | tf_op jit(solution)/shard_map/ppermute | solution.py:11
  105.9 5.6 %collective-permute-done.31 = bf16[48,1792]{1,0:T(8,128)(2,1)S(1)} collective-permute-done((bf16[48,1792]{1,0:T(8,128)(2,1)S(1)}, bf16[48,1792]{1,0:T(8,128)(2,1)S(1)}, u32[]{:S(2)}, u32[]{:S(2)}) %collective-permute-start.31) | collective-permute-done | bytes 172064 | tf_op jit(solution)/shard_map/ppermute | solution.py:11
  115.5 1.7 collective-permute-done.43
  118.4 1.7 fusion
  120.1 5.8 %collective-permute-done.18 = bf16[192,512]{1,0:T(8,128)(2,1)S(1)} collective-permute-done((bf16[192,512]{1,0:T(8,128)(2,1)S(1)}, bf16[192,512]{1,0:T(8,128)(2,1)S(1)}, u32[]{:S(2)}, u32[]{:S(2)}) %collective-permute-start.18) | collective-permute-done | bytes 196640 | tf_op jit(solution)/shard_map/ppermute | solution.py:11
  126.0 1.7 fusion.15
  130.8 2.2 collective-permute-start.51
  136.2 4.2 %collective-permute-done.54 = bf16[192,256]{1,0:T(8,128)(2,1)S(1)} collective-permute-done((bf16[192,256]{1,0:T(8,128)(2,1)S(1)}, bf16[192,256]{1,0:T(8,128)(2,1)S(1)}, u32[]{:S(2)}, u32[]{:S(2)}) %collective-permute-start.54) | collective-permute-done | bytes 98336 | tf_op jit(solution)/shard_map/ppermute | solution.py:11
  141.4 3.6 %collective-permute-done.52 = bf16[192,256]{1,0:T(8,128)(2,1)S(1)} collective-permute-done((bf16[192,256]{1,0:T(8,128)(2,1)S(1)}, bf16[192,256]{1,0:T(8,128)(2,1)S(1)}, u32[]{:S(2)}, u32[]{:S(2)}) %collective-permute-start.52) | collective-permute-done | bytes 98336 | tf_op jit(solution)/shard_map/ppermute | solution.py:11
  146.2 1.5 collective-permute-start.57
  149.9 1.8 collective-permute-done.57
  155.4 6.5 %collective-permute-done.59 = bf16[192,512]{1,0:T(8,128)(2,1)S(1)} collective-permute-done((bf16[192,512]{1,0:T(8,128)(2,1)S(1)}, bf16[192,512]{1,0:T(8,128)(2,1)S(1)}, u32[]{:S(2)}, u32[]{:S(2)}) %collective-permute-start.59) | collective-permute-done | bytes 196640 | tf_op jit(solution)/shard_map/ppermute | solution.py:11
  163.7 9.4 %collective-permute-done.60 = bf16[192,512]{1,0:T(8,128)(2,1)S(1)} collective-permute-done((bf16[192,512]{1,0:T(8,128)(2,1)S(1)}, bf16[192,512]{1,0:T(8,128)(2,1)S(1)}, u32[]{:S(2)}, u32[]{:S(2)}) %collective-permute-start.60) | collective-permute-done | bytes 196640 | tf_op jit(solution)/shard_map/ppermute | solution.py:11
  174.7 3.6 %convolution_convert_fusion = bf16[192,1792]{1,0:T(8,128)(2,1)S(1)} fusion(bf16[1792,1024]{1,0:T(8,128)(2,1)} %param.16, bf16[192,512]{1,0:T(8,128)(2,1)} %collective-permute-done.61, bf16[192,512]{1,0:T(8,128)(2,1)S(1)} %add_convert_fusion, pred[]{:T(512)S(6)} %eq.24), kind=kOutput, calls=%fused_computation.18 | convolution fusion | flops 706756608 | bytes 4751361 | tf_op jit(solution)/shard_map/dot_general | solution.py:19
  182.7 2.8 %fusion.45 = f32[1024,1024]{0,1:T(8,128)} fusion(bf16[192,256]{1,0:T(8,128)(2,1)S(1)} %bitcast.41, bf16[192,256]{1,0:T(8,128)(2,1)S(1)} %bitcast.39, bf16[192,256]{1,0:T(8,128)(2,1)S(1)} %bitcast.40, bf16[192,256]{1,0:T(8,128)(2,1)S(1)} %bitcast.38, bf16[192,512]{1,0:T(8,128)(2,1)S(1)} %copy-done.14, bf16[192,512]{1,0:T(8,128)(2,1)S(1)} %add_convert_fusion.3, ...), kind=kOutput, calls=%fused_computation.61 | convolution fusion | flops 405995520 | bytes 4980737 | tf_op jit(solution)/shard_map/dot_general | solution.py:23
  185.5 5.3 %copy.23 = f32[1024,4,256]{2,1,0:T(4,128)} copy(f32[1024,4,256]{0,2,1:T(8,128)} %bitcast.37) | data formatting | bytes 8388608
  194.2 1.5 collective-permute-start.69
  197.5 5.4 %fusion.103 = f32[1792,1024]{1,0:T(8,128)} fusion(bf16[48,1792]{1,0:T(8,128)(2,1)S(1)} %copy-done.16, bf16[48,1792]{1,0:T(8,128)(2,1)S(1)} %copy-done.18, bf16[48,1792]{1,0:T(8,128)(2,1)S(1)} %copy-done.20, bf16[48,1792]{1,0:T(8,128)(2,1)S(1)} %copy-done.10, bf16[192,512]{1,0:T(8,128)(2,1)} %collective-permute-done.61, ...), kind=kOutput, calls=%fused_computation.148 | convolution fusion | flops 709165056 | bytes 8421377 | tf_op jit(solution)/shard_map/dot_general | solution.py:23
  206.0 1.6 collective-permute-done.70
  211.7 2.7 %collective-permute-done.68 = bf16[48,1792]{1,0:T(8,128)(2,1)S(1)} collective-permute-done((bf16[48,1792]{1,0:T(8,128)(2,1)S(1)}, bf16[48,1792]{1,0:T(8,128)(2,1)S(1)}, u32[]{:S(2)}, u32[]{:S(2)}) %collective-permute-start.68) | collective-permute-done | bytes 172064 | tf_op jit(solution)/shard_map/ppermute | solution.py:11
  214.4 2.8 %collective-permute-done.67 = bf16[48,1792]{1,0:T(8,128)(2,1)S(1)} collective-permute-done((bf16[48,1792]{1,0:T(8,128)(2,1)S(1)}, bf16[48,1792]{1,0:T(8,128)(2,1)S(1)}, u32[]{:S(2)}, u32[]{:S(2)}) %collective-permute-start.67) | collective-permute-done | bytes 172064 | tf_op jit(solution)/shard_map/ppermute | solution.py:11
  218.8 3.6 %convolution_convert_fusion.4 = bf16[256,1024]{1,0:T(8,128)(2,1)S(1)} fusion(f32[192,1024]{1,0:T(8,128)S(1)} %fusion.102, bf16[1024,1792]{1,0:T(8,128)(2,1)} %param.15, s32[]{:T(128)S(6)} %axis_index.25, s32[256]{0:T(256)S(1)} %get-tuple-element.107, s32[256]{0:T(256)S(1)} %get-tuple-element.108, s32[]{:T(128)S(6)} %axis_index.22, ...), kind=kOutput, calls=%fused_computation.23 | convolution fusion | flops 809844736 | bytes 5673480 | tf_op jit(solution)/shard_map/dot_general | solution.py:15
  223.1 4.2 %fusion.100 = f32[1024,1792]{1,0:T(8,128)} fusion(bf16[192,1024]{1,0:T(8,128)(2,1)S(1)} %convolution_convert_fusion.7, bf16[48,1792]{1,0:T(8,128)(2,1)S(1)} %get-tuple-element.70, bf16[48,1792]{1,0:T(8,128)(2,1)S(1)} %get-tuple-element.68, bf16[48,1792]{1,0:T(8,128)(2,1)S(1)} %get-tuple-element.66, bf16[48,1792]{1,0:T(8,128)(2,1)S(1)} %get-tuple-element.15), kind=kOutput, calls=%fused_computation.145 | convolution fusion | flops 707395584 | bytes 8421376 | tf_op jit(solution)/shard_map/dot_general | solution.py:23
  227.9 2.2 collective-permute-start.80
  231.4 4.2 %fusion.101 = f32[1024,1792]{1,0:T(8,128)} fusion(bf16[192,1024]{1,0:T(8,128)(2,1)S(1)} %convolution_convert_fusion.7, bf16[48,1792]{1,0:T(8,128)(2,1)S(1)} %get-tuple-element.71, bf16[48,1792]{1,0:T(8,128)(2,1)S(1)} %get-tuple-element.69, bf16[48,1792]{1,0:T(8,128)(2,1)S(1)} %get-tuple-element.67, bf16[48,1792]{1,0:T(8,128)(2,1)S(1)} %get-tuple-element.18), kind=kOutput, calls=%fused_computation.146 | convolution fusion | flops 707395584 | bytes 8421376 | tf_op jit(solution)/shard_map/dot_general | solution.py:23
  (275 shorter events, 83.9 us)
Async XLA Ops:
  0.6 25.0 %collective-permute-start.3 = (bf16[24,1024]{1,0:T(8,128)(2,1)}, bf16[24,1024]{1,0:T(8,128)(2,1)}, u32[]{:S(2)}, u32[]{:S(2)}) collective-permute-start(bf16[24,1024]{1,0:T(8,128)(2,1)} %param.13), channel_id=1, source_target_pairs={{0,4},{1,5},{2,6},{3,7},{4,0},{5,1},{6,2},{7,3},{8,12},{9,13},{10,... | collective-permute-start | bytes 147464 | tf_op jit(solution)/shard_map/ppermute | solution.py:11
  4.8 16.2 %collective-permute-start.1 = (bf16[24,1024]{1,0:T(8,128)(2,1)}, bf16[24,1024]{1,0:T(8,128)(2,1)}, u32[]{:S(2)}, u32[]{:S(2)}) collective-permute-start(bf16[24,1024]{1,0:T(8,128)(2,1)} %param.13), channel_id=1, source_target_pairs={{0,2},{1,3},{2,0},{3,1},{4,6},{5,7},{6,4},{7,5},{8,10},{9,11},{10,... | collective-permute-start | bytes 147464 | tf_op jit(solution)/shard_map/ppermute | solution.py:11
  6.3 17.2 %collective-permute-start = (bf16[24,1024]{1,0:T(8,128)(2,1)}, bf16[24,1024]{1,0:T(8,128)(2,1)S(1)}, u32[]{:S(2)}, u32[]{:S(2)}) collective-permute-start(bf16[24,1024]{1,0:T(8,128)(2,1)} %param.13), channel_id=1, source_target_pairs={{0,1},{1,0},{2,3},{3,2},{4,5},{5,4},{6,7},{7,6},{8,9},{9,8},{10,11... | collective-permute-start | bytes 147464 | tf_op jit(solution)/shard_map/ppermute | solution.py:11
  6.3 21.9 %collective-permute-start.5 = (bf16[24,1024]{1,0:T(8,128)(2,1)}, bf16[24,1024]{1,0:T(8,128)(2,1)S(1)}, u32[]{:S(2)}, u32[]{:S(2)}) collective-permute-start(bf16[24,1024]{1,0:T(8,128)(2,1)} %param.13), channel_id=1, source_target_pairs={{0,6},{1,7},{2,4},{3,5},{4,2},{5,3},{6,0},{7,1},{8,14},{9,15},{10,... | collective-permute-start | bytes 147464 | tf_op jit(solution)/shard_map/ppermute | solution.py:11
  6.3 33.0 %collective-permute-start.23 = (bf16[24,2048]{1,0:T(8,128)(2,1)}, bf16[24,2048]{1,0:T(8,128)(2,1)S(1)}, u32[]{:S(2)}, u32[]{:S(2)}) collective-permute-start(bf16[24,2048]{1,0:T(8,128)(2,1)} %param.9), channel_id=1, source_target_pairs={{0,4},{1,5},{2,6},{3,7},{4,0},{5,1},{6,2},{7,3},{8,12},{9,13},{10,... | collective-permute-start | bytes 294920 | tf_op jit(solution)/shard_map/ppermute | solution.py:11
  21.0 16.7 %collective-permute-start.21 = (bf16[24,2048]{1,0:T(8,128)(2,1)S(1)}, bf16[24,2048]{1,0:T(8,128)(2,1)S(1)}, u32[]{:S(2)}, u32[]{:S(2)}) collective-permute-start(bf16[24,2048]{1,0:T(8,128)(2,1)S(1)} %copy-done.21), channel_id=1, source_target_pairs={{0,2},{1,3},{2,0},{3,1},{4,6},{5,7},{6,4},{7,5},{8,10},{9,11},{10,... | collective-permute-start | bytes 294920 | tf_op jit(solution)/shard_map/ppermute | solution.py:11
  25.6 13.7 %collective-permute-start.20 = (bf16[24,2048]{1,0:T(8,128)(2,1)S(1)}, bf16[24,2048]{1,0:T(8,128)(2,1)S(1)}, u32[]{:S(2)}, u32[]{:S(2)}) collective-permute-start(bf16[24,2048]{1,0:T(8,128)(2,1)S(1)} %copy-done.21), channel_id=1, source_target_pairs={{0,1},{1,0},{2,3},{3,2},{4,5},{5,4},{6,7},{7,6},{8,9},{9,8},{10,11... | collective-permute-start | bytes 294920 | tf_op jit(solution)/shard_map/ppermute | solution.py:11
  28.2 12.5 %collective-permute-start.25 = (bf16[24,2048]{1,0:T(8,128)(2,1)S(1)}, bf16[24,2048]{1,0:T(8,128)(2,1)S(1)}, u32[]{:S(2)}, u32[]{:S(2)}) collective-permute-start(bf16[24,2048]{1,0:T(8,128)(2,1)S(1)} %copy-done.21), channel_id=1, source_target_pairs={{0,6},{1,7},{2,4},{3,5},{4,2},{5,3},{6,0},{7,1},{8,14},{9,15},{10,... | collective-permute-start | bytes 294920 | tf_op jit(solution)/shard_map/ppermute | solution.py:11
  35.2 25.3 %collective-permute-start.7 = (bf16[48,1792]{1,0:T(8,128)(2,1)S(1)}, bf16[48,1792]{1,0:T(8,128)(2,1)S(1)}, u32[]{:S(2)}, u32[]{:S(2)}) collective-permute-start(bf16[48,1792]{1,0:T(8,128)(2,1)S(1)} %get-tuple-element.49), channel_id=1, source_target_pairs={{0,8},{8,0},{16,24},{24,16},{1,9},{9,1},{17,25},{25,17},{2,10},{10... | collective-permute-start | bytes 516104 | tf_op jit(solution)/shard_map/ppermute | solution.py:11
  37.7 24.1 %collective-permute-start.9 = (bf16[48,1792]{1,0:T(8,128)(2,1)S(1)}, bf16[48,1792]{1,0:T(8,128)(2,1)S(1)}, u32[]{:S(2)}, u32[]{:S(2)}) collective-permute-start(bf16[48,1792]{1,0:T(8,128)(2,1)S(1)} %get-tuple-element.50), channel_id=1, source_target_pairs={{0,24},{8,16},{16,8},{24,0},{1,25},{9,17},{17,9},{25,1},{2,26},{10... | collective-permute-start | bytes 516104 | tf_op jit(solution)/shard_map/ppermute | solution.py:11
  39.3 23.5 %collective-permute-start.8 = (bf16[48,1792]{1,0:T(8,128)(2,1)S(1)}, bf16[48,1792]{1,0:T(8,128)(2,1)S(1)}, u32[]{:S(2)}, u32[]{:S(2)}) collective-permute-start(bf16[48,1792]{1,0:T(8,128)(2,1)S(1)} %get-tuple-element.51), channel_id=1, source_target_pairs={{0,16},{8,24},{16,0},{24,8},{1,17},{9,25},{17,1},{25,9},{2,18},{10... | collective-permute-start | bytes 516104 | tf_op jit(solution)/shard_map/ppermute | solution.py:11
  40.8 23.4 %collective-permute-start.10 = (bf16[48,1792]{1,0:T(8,128)(2,1)S(1)}, bf16[48,1792]{1,0:T(8,128)(2,1)S(1)}, u32[]{:S(2)}, u32[]{:S(2)}) collective-permute-start(bf16[48,1792]{1,0:T(8,128)(2,1)S(1)} %get-tuple-element.46), channel_id=1, source_target_pairs={{0,8},{8,0},{16,24},{24,16},{1,9},{9,1},{17,25},{25,17},{2,10},{10... | collective-permute-start | bytes 516104 | tf_op jit(solution)/shard_map/ppermute | solution.py:11
  43.6 20.6 %collective-permute-start.12 = (bf16[48,1792]{1,0:T(8,128)(2,1)S(1)}, bf16[48,1792]{1,0:T(8,128)(2,1)S(1)}, u32[]{:S(2)}, u32[]{:S(2)}) collective-permute-start(bf16[48,1792]{1,0:T(8,128)(2,1)S(1)} %get-tuple-element.47), channel_id=1, source_target_pairs={{0,24},{8,16},{16,8},{24,0},{1,25},{9,17},{17,9},{25,1},{2,26},{10... | collective-permute-start | bytes 516104 | tf_op jit(solution)/shard_map/ppermute | solution.py:11
  61.8 21.1 %collective-permute-start.39 = (bf16[48,1792]{1,0:T(8,128)(2,1)S(1)}, bf16[48,1792]{1,0:T(8,128)(2,1)S(1)}, u32[]{:S(2)}, u32[]{:S(2)}) collective-permute-start(bf16[48,1792]{1,0:T(8,128)(2,1)S(1)} %get-tuple-element.43), channel_id=1, source_target_pairs={{0,8},{8,0},{16,24},{24,16},{1,9},{9,1},{17,25},{25,17},{2,10},{10... | collective-permute-start | bytes 516104 | tf_op jit(solution)/shard_map/ppermute | solution.py:11
  62.8 21.1 %collective-permute-start.41 = (bf16[48,1792]{1,0:T(8,128)(2,1)S(1)}, bf16[48,1792]{1,0:T(8,128)(2,1)S(1)}, u32[]{:S(2)}, u32[]{:S(2)}) collective-permute-start(bf16[48,1792]{1,0:T(8,128)(2,1)S(1)} %get-tuple-element.44), channel_id=1, source_target_pairs={{0,24},{8,16},{16,8},{24,0},{1,25},{9,17},{17,9},{25,1},{2,26},{10... | collective-permute-start | bytes 516104 | tf_op jit(solution)/shard_map/ppermute | solution.py:11
  67.1 9.8 %collective-permute-start.15 = (bf16[48,1792]{1,0:T(8,128)(2,1)S(1)}, bf16[48,1792]{1,0:T(8,128)(2,1)S(1)}, u32[]{:S(2)}, u32[]{:S(2)}) collective-permute-start(bf16[48,1792]{1,0:T(8,128)(2,1)S(1)} %multiply_convert_fusion.3), channel_id=1, source_target_pairs={{0,24},{8,16},{16,8},{24,0},{1,25},{9,17},{17,9},{25,1},{2,26},{10... | collective-permute-start | bytes 516104 | tf_op jit(solution)/shard_map/ppermute | solution.py:11
  68.7 10.5 %collective-permute-start.14 = (bf16[48,1792]{1,0:T(8,128)(2,1)S(1)}, bf16[48,1792]{1,0:T(8,128)(2,1)S(1)}, u32[]{:S(2)}, u32[]{:S(2)}) collective-permute-start(bf16[48,1792]{1,0:T(8,128)(2,1)S(1)} %multiply_convert_fusion.3), channel_id=1, source_target_pairs={{0,16},{8,24},{16,0},{24,8},{1,17},{9,25},{17,1},{25,9},{2,18},{10... | collective-permute-start | bytes 516104 | tf_op jit(solution)/shard_map/ppermute | solution.py:11
  69.6 10.6 %collective-permute-start.13 = (bf16[48,1792]{1,0:T(8,128)(2,1)S(1)}, bf16[48,1792]{1,0:T(8,128)(2,1)S(1)}, u32[]{:S(2)}, u32[]{:S(2)}) collective-permute-start(bf16[48,1792]{1,0:T(8,128)(2,1)S(1)} %multiply_convert_fusion.3), channel_id=1, source_target_pairs={{0,8},{8,0},{16,24},{24,16},{1,9},{9,1},{17,25},{25,17},{2,10},{10... | collective-permute-start | bytes 516104 | tf_op jit(solution)/shard_map/ppermute | solution.py:11
  80.2 10.5 %collective-permute-start.38 = (bf16[48,1792]{1,0:T(8,128)(2,1)S(1)}, bf16[48,1792]{1,0:T(8,128)(2,1)S(1)}, u32[]{:S(2)}, u32[]{:S(2)}) collective-permute-start(bf16[48,1792]{1,0:T(8,128)(2,1)S(1)} %get-tuple-element.41), channel_id=1, source_target_pairs={{0,24},{8,16},{16,8},{24,0},{1,25},{9,17},{17,9},{25,1},{2,26},{10... | collective-permute-start | bytes 516104 | tf_op jit(solution)/shard_map/ppermute | solution.py:11
  82.9 10.9 %collective-permute-start.37 = (bf16[48,1792]{1,0:T(8,128)(2,1)S(1)}, bf16[48,1792]{1,0:T(8,128)(2,1)S(1)}, u32[]{:S(2)}, u32[]{:S(2)}) collective-permute-start(bf16[48,1792]{1,0:T(8,128)(2,1)S(1)} %get-tuple-element.42), channel_id=1, source_target_pairs={{0,16},{8,24},{16,0},{24,8},{1,17},{9,25},{17,1},{25,9},{2,18},{10... | collective-permute-start | bytes 516104 | tf_op jit(solution)/shard_map/ppermute | solution.py:11
  83.9 10.2 %collective-permute-start.27 = (bf16[48,1792]{1,0:T(8,128)(2,1)S(1)}, bf16[48,1792]{1,0:T(8,128)(2,1)S(1)}, u32[]{:S(2)}, u32[]{:S(2)}) collective-permute-start(bf16[48,1792]{1,0:T(8,128)(2,1)S(1)} %get-tuple-element.34), channel_id=1, source_target_pairs={{0,8},{8,0},{16,24},{24,16},{1,9},{9,1},{17,25},{25,17},{2,10},{10... | collective-permute-start | bytes 516104 | tf_op jit(solution)/shard_map/ppermute | solution.py:11
  85.0 13.2 %collective-permute-start.29 = (bf16[48,1792]{1,0:T(8,128)(2,1)S(1)}, bf16[48,1792]{1,0:T(8,128)(2,1)S(1)}, u32[]{:S(2)}, u32[]{:S(2)}) collective-permute-start(bf16[48,1792]{1,0:T(8,128)(2,1)S(1)} %get-tuple-element.35), channel_id=1, source_target_pairs={{0,24},{8,16},{16,8},{24,0},{1,25},{9,17},{17,9},{25,1},{2,26},{10... | collective-permute-start | bytes 516104 | tf_op jit(solution)/shard_map/ppermute | solution.py:11
  86.6 14.6 %collective-permute-start.28 = (bf16[48,1792]{1,0:T(8,128)(2,1)S(1)}, bf16[48,1792]{1,0:T(8,128)(2,1)S(1)}, u32[]{:S(2)}, u32[]{:S(2)}) collective-permute-start(bf16[48,1792]{1,0:T(8,128)(2,1)S(1)} %get-tuple-element.36), channel_id=1, source_target_pairs={{0,16},{8,24},{16,0},{24,8},{1,17},{9,25},{17,1},{25,9},{2,18},{10... | collective-permute-start | bytes 516104 | tf_op jit(solution)/shard_map/ppermute | solution.py:11
  90.8 11.3 %collective-permute-start.30 = (bf16[48,1792]{1,0:T(8,128)(2,1)S(1)}, bf16[48,1792]{1,0:T(8,128)(2,1)S(1)}, u32[]{:S(2)}, u32[]{:S(2)}) collective-permute-start(bf16[48,1792]{1,0:T(8,128)(2,1)S(1)} %get-tuple-element.37), channel_id=1, source_target_pairs={{0,8},{8,0},{16,24},{24,16},{1,9},{9,1},{17,25},{25,17},{2,10},{10... | collective-permute-start | bytes 516104 | tf_op jit(solution)/shard_map/ppermute | solution.py:11
  94.1 11.6 %collective-permute-start.32 = (bf16[48,1792]{1,0:T(8,128)(2,1)S(1)}, bf16[48,1792]{1,0:T(8,128)(2,1)S(1)}, u32[]{:S(2)}, u32[]{:S(2)}) collective-permute-start(bf16[48,1792]{1,0:T(8,128)(2,1)S(1)} %get-tuple-element.38), channel_id=1, source_target_pairs={{0,24},{8,16},{16,8},{24,0},{1,25},{9,17},{17,9},{25,1},{2,26},{10... | collective-permute-start | bytes 516104 | tf_op jit(solution)/shard_map/ppermute | solution.py:11
  95.5 16.0 %collective-permute-start.31 = (bf16[48,1792]{1,0:T(8,128)(2,1)S(1)}, bf16[48,1792]{1,0:T(8,128)(2,1)S(1)}, u32[]{:S(2)}, u32[]{:S(2)}) collective-permute-start(bf16[48,1792]{1,0:T(8,128)(2,1)S(1)} %get-tuple-element.39), channel_id=1, source_target_pairs={{0,16},{8,24},{16,0},{24,8},{1,17},{9,25},{17,1},{25,9},{2,18},{10... | collective-permute-start | bytes 516104 | tf_op jit(solution)/shard_map/ppermute | solution.py:11
  98.2 16.2 %collective-permute-start.44 = (bf16[48,1792]{1,0:T(8,128)(2,1)S(1)}, bf16[48,1792]{1,0:T(8,128)(2,1)S(1)}, u32[]{:S(2)}, u32[]{:S(2)}) collective-permute-start(bf16[48,1792]{1,0:T(8,128)(2,1)S(1)} %multiply_convert_fusion.1), channel_id=1, source_target_pairs={{0,24},{8,16},{16,8},{24,0},{1,25},{9,17},{17,9},{25,1},{2,26},{10... | collective-permute-start | bytes 516104 | tf_op jit(solution)/shard_map/ppermute | solution.py:11
  101.2 16.0 %collective-permute-start.43 = (bf16[48,1792]{1,0:T(8,128)(2,1)S(1)}, bf16[48,1792]{1,0:T(8,128)(2,1)S(1)}, u32[]{:S(2)}, u32[]{:S(2)}) collective-permute-start(bf16[48,1792]{1,0:T(8,128)(2,1)S(1)} %multiply_convert_fusion.1), channel_id=1, source_target_pairs={{0,16},{8,24},{16,0},{24,8},{1,17},{9,25},{17,1},{25,9},{2,18},{10... | collective-permute-start | bytes 516104 | tf_op jit(solution)/shard_map/ppermute | solution.py:11
  102.1 16.3 %collective-permute-start.42 = (bf16[48,1792]{1,0:T(8,128)(2,1)S(1)}, bf16[48,1792]{1,0:T(8,128)(2,1)S(1)}, u32[]{:S(2)}, u32[]{:S(2)}) collective-permute-start(bf16[48,1792]{1,0:T(8,128)(2,1)S(1)} %multiply_convert_fusion.1), channel_id=1, source_target_pairs={{0,8},{8,0},{16,24},{24,16},{1,9},{9,1},{17,25},{25,17},{2,10},{10... | collective-permute-start | bytes 516104 | tf_op jit(solution)/shard_map/ppermute | solution.py:11
  111.8 14.2 %collective-permute-start.35 = (bf16[48,1792]{1,0:T(8,128)(2,1)S(1)}, bf16[48,1792]{1,0:T(8,128)(2,1)S(1)}, u32[]{:S(2)}, u32[]{:S(2)}) collective-permute-start(bf16[48,1792]{1,0:T(8,128)(2,1)S(1)} %multiply_convert_fusion.2), channel_id=1, source_target_pairs={{0,24},{8,16},{16,8},{24,0},{1,25},{9,17},{17,9},{25,1},{2,26},{10... | collective-permute-start | bytes 516104 | tf_op jit(solution)/shard_map/ppermute | solution.py:11
  113.2 12.8 %collective-permute-start.34 = (bf16[48,1792]{1,0:T(8,128)(2,1)S(1)}, bf16[48,1792]{1,0:T(8,128)(2,1)S(1)}, u32[]{:S(2)}, u32[]{:S(2)}) collective-permute-start(bf16[48,1792]{1,0:T(8,128)(2,1)S(1)} %multiply_convert_fusion.2), channel_id=1, source_target_pairs={{0,16},{8,24},{16,0},{24,8},{1,17},{9,25},{17,1},{25,9},{2,18},{10... | collective-permute-start | bytes 516104 | tf_op jit(solution)/shard_map/ppermute | solution.py:11
  114.4 11.6 %collective-permute-start.33 = (bf16[48,1792]{1,0:T(8,128)(2,1)S(1)}, bf16[48,1792]{1,0:T(8,128)(2,1)S(1)}, u32[]{:S(2)}, u32[]{:S(2)}) collective-permute-start(bf16[48,1792]{1,0:T(8,128)(2,1)S(1)} %multiply_convert_fusion.2), channel_id=1, source_target_pairs={{0,8},{8,0},{16,24},{24,16},{1,9},{9,1},{17,25},{25,17},{2,10},{10... | collective-permute-start | bytes 516104 | tf_op jit(solution)/shard_map/ppermute | solution.py:11
  117.2 8.7 %collective-permute-start.18 = (bf16[192,512]{1,0:T(8,128)(2,1)S(1)}, bf16[192,512]{1,0:T(8,128)(2,1)S(1)}, u32[]{:S(2)}, u32[]{:S(2)}) collective-permute-start(bf16[192,512]{1,0:T(8,128)(2,1)S(1)} %add_convert_fusion.4), channel_id=1, source_target_pairs={{0,4},{1,5},{2,6},{3,7},{4,0},{5,1},{6,2},{7,3},{8,12},{9,13},{10,... | collective-permute-start | bytes 589832 | tf_op jit(solution)/shard_map/ppermute | solution.py:11
  127.8 17.2 %collective-permute-start.45 = (bf16[192,256]{1,0:T(8,128)(2,1)S(1)}, bf16[192,256]{1,0:T(8,128)(2,1)S(1)}, u32[]{:S(2)}, u32[]{:S(2)}) collective-permute-start(bf16[192,256]{1,0:T(8,128)(2,1)S(1)} %get-tuple-element.24), channel_id=1, source_target_pairs={{0,1},{1,0},{2,3},{3,2},{4,5},{5,4},{6,7},{7,6},{8,9},{9,8},{10,11... | collective-permute-start | bytes 294920 | tf_op jit(solution)/shard_map/ppermute | solution.py:11
  130.7 14.2 %collective-permute-start.47 = (bf16[192,256]{1,0:T(8,128)(2,1)S(1)}, bf16[192,256]{1,0:T(8,128)(2,1)S(1)}, u32[]{:S(2)}, u32[]{:S(2)}) collective-permute-start(bf16[192,256]{1,0:T(8,128)(2,1)S(1)} %get-tuple-element.28), channel_id=1, source_target_pairs={{0,2},{1,3},{2,0},{3,1},{4,6},{5,7},{6,4},{7,5},{8,10},{9,11},{10,... | collective-permute-start | bytes 294920 | tf_op jit(solution)/shard_map/ppermute | solution.py:11
  130.8 14.2 %collective-permute-start.51 = (bf16[192,256]{1,0:T(8,128)(2,1)S(1)}, bf16[192,256]{1,0:T(8,128)(2,1)S(1)}, u32[]{:S(2)}, u32[]{:S(2)}) collective-permute-start(bf16[192,256]{1,0:T(8,128)(2,1)S(1)} %get-tuple-element.29), channel_id=1, source_target_pairs={{0,6},{1,7},{2,4},{3,5},{4,2},{5,3},{6,0},{7,1},{8,14},{9,15},{10,... | collective-permute-start | bytes 294920 | tf_op jit(solution)/shard_map/ppermute | solution.py:11
  133.0 12.0 %collective-permute-start.49 = (bf16[192,256]{1,0:T(8,128)(2,1)S(1)}, bf16[192,256]{1,0:T(8,128)(2,1)S(1)}, u32[]{:S(2)}, u32[]{:S(2)}) collective-permute-start(bf16[192,256]{1,0:T(8,128)(2,1)S(1)} %get-tuple-element.30), channel_id=1, source_target_pairs={{0,4},{1,5},{2,6},{3,7},{4,0},{5,1},{6,2},{7,3},{8,12},{9,13},{10,... | collective-permute-start | bytes 294920 | tf_op jit(solution)/shard_map/ppermute | solution.py:11
  161.9 11.1 %collective-permute-start.60 = (bf16[192,512]{1,0:T(8,128)(2,1)S(1)}, bf16[192,512]{1,0:T(8,128)(2,1)S(1)}, u32[]{:S(2)}, u32[]{:S(2)}) collective-permute-start(bf16[192,512]{1,0:T(8,128)(2,1)S(1)} %add_convert_fusion.1), channel_id=1, source_target_pairs={{0,4},{1,5},{2,6},{3,7},{4,0},{5,1},{6,2},{7,3},{8,12},{9,13},{10,... | collective-permute-start | bytes 589832 | tf_op jit(solution)/shard_map/ppermute | solution.py:11
  179.2 11.6 %collective-permute-start.62 = (bf16[48,1792]{1,0:T(8,128)(2,1)}, bf16[48,1792]{1,0:T(8,128)(2,1)S(1)}, u32[]{:S(2)}, u32[]{:S(2)}) collective-permute-start(bf16[48,1792]{1,0:T(8,128)(2,1)} %get-tuple-element.31), channel_id=1, source_target_pairs={{0,8},{8,0},{16,24},{24,16},{1,9},{9,1},{17,25},{25,17},{2,10},{10... | collective-permute-start | bytes 516104 | tf_op jit(solution)/shard_map/ppermute | solution.py:11
  180.2 10.6 %collective-permute-start.64 = (bf16[48,1792]{1,0:T(8,128)(2,1)}, bf16[48,1792]{1,0:T(8,128)(2,1)S(1)}, u32[]{:S(2)}, u32[]{:S(2)}) collective-permute-start(bf16[48,1792]{1,0:T(8,128)(2,1)} %get-tuple-element.32), channel_id=1, source_target_pairs={{0,24},{8,16},{16,8},{24,0},{1,25},{9,17},{17,9},{25,1},{2,26},{10... | collective-permute-start | bytes 516104 | tf_op jit(solution)/shard_map/ppermute | solution.py:11
  181.7 9.8 %collective-permute-start.63 = (bf16[48,1792]{1,0:T(8,128)(2,1)S(1)}, bf16[48,1792]{1,0:T(8,128)(2,1)}, u32[]{:S(2)}, u32[]{:S(2)}) collective-permute-start(bf16[48,1792]{1,0:T(8,128)(2,1)S(1)} %get-tuple-element.33), channel_id=1, source_target_pairs={{0,16},{8,24},{16,0},{24,8},{1,17},{9,25},{17,1},{25,9},{2,18},{10... | collective-permute-start | bytes 516104 | tf_op jit(solution)/shard_map/ppermute | solution.py:11
  192.7 12.3 %collective-permute-start.73 = (bf16[48,1792]{1,0:T(8,128)(2,1)S(1)}, bf16[48,1792]{1,0:T(8,128)(2,1)S(1)}, u32[]{:S(2)}, u32[]{:S(2)}) collective-permute-start(bf16[48,1792]{1,0:T(8,128)(2,1)S(1)} %get-tuple-element.16), channel_id=1, source_target_pairs={{0,24},{8,16},{16,8},{24,0},{1,25},{9,17},{17,9},{25,1},{2,26},{10... | collective-permute-start | bytes 516104 | tf_op jit(solution)/shard_map/ppermute | solution.py:11
  194.2 14.3 %collective-permute-start.69 = (bf16[48,1792]{1,0:T(8,128)(2,1)S(1)}, bf16[48,1792]{1,0:T(8,128)(2,1)S(1)}, u32[]{:S(2)}, u32[]{:S(2)}) collective-permute-start(bf16[48,1792]{1,0:T(8,128)(2,1)S(1)} %get-tuple-element.17), channel_id=1, source_target_pairs={{0,24},{8,16},{16,8},{24,0},{1,25},{9,17},{17,9},{25,1},{2,26},{10... | collective-permute-start | bytes 516104 | tf_op jit(solution)/shard_map/ppermute | solution.py:11
  196.0 11.6 %collective-permute-start.70 = (bf16[48,1792]{1,0:T(8,128)(2,1)S(1)}, bf16[48,1792]{1,0:T(8,128)(2,1)S(1)}, u32[]{:S(2)}, u32[]{:S(2)}) collective-permute-start(bf16[48,1792]{1,0:T(8,128)(2,1)S(1)} %get-tuple-element.19), channel_id=1, source_target_pairs={{0,24},{8,16},{16,8},{24,0},{1,25},{9,17},{17,9},{25,1},{2,26},{10... | collective-permute-start | bytes 516104 | tf_op jit(solution)/shard_map/ppermute | solution.py:11
  204.0 13.4 %collective-permute-start.71 = (bf16[48,1792]{1,0:T(8,128)(2,1)S(1)}, bf16[48,1792]{1,0:T(8,128)(2,1)S(1)}, u32[]{:S(2)}, u32[]{:S(2)}) collective-permute-start(bf16[48,1792]{1,0:T(8,128)(2,1)S(1)} %get-tuple-element.16), channel_id=1, source_target_pairs={{0,8},{8,0},{16,24},{24,16},{1,9},{9,1},{17,25},{25,17},{2,10},{10... | collective-permute-start | bytes 516104 | tf_op jit(solution)/shard_map/ppermute | solution.py:11
  205.0 9.4 %collective-permute-start.68 = (bf16[48,1792]{1,0:T(8,128)(2,1)S(1)}, bf16[48,1792]{1,0:T(8,128)(2,1)S(1)}, u32[]{:S(2)}, u32[]{:S(2)}) collective-permute-start(bf16[48,1792]{1,0:T(8,128)(2,1)S(1)} %get-tuple-element.19), channel_id=1, source_target_pairs={{0,16},{8,24},{16,0},{24,8},{1,17},{9,25},{17,1},{25,9},{2,18},{10... | collective-permute-start | bytes 516104 | tf_op jit(solution)/shard_map/ppermute | solution.py:11
  207.6 9.7 %collective-permute-start.66 = (bf16[48,1792]{1,0:T(8,128)(2,1)S(1)}, bf16[48,1792]{1,0:T(8,128)(2,1)S(1)}, u32[]{:S(2)}, u32[]{:S(2)}) collective-permute-start(bf16[48,1792]{1,0:T(8,128)(2,1)S(1)} %get-tuple-element.19), channel_id=1, source_target_pairs={{0,8},{8,0},{16,24},{24,16},{1,9},{9,1},{17,25},{25,17},{2,10},{10... | collective-permute-start | bytes 516104 | tf_op jit(solution)/shard_map/ppermute | solution.py:11
  208.5 8.7 %collective-permute-start.67 = (bf16[48,1792]{1,0:T(8,128)(2,1)S(1)}, bf16[48,1792]{1,0:T(8,128)(2,1)S(1)}, u32[]{:S(2)}, u32[]{:S(2)}) collective-permute-start(bf16[48,1792]{1,0:T(8,128)(2,1)S(1)} %get-tuple-element.17), channel_id=1, source_target_pairs={{0,16},{8,24},{16,0},{24,8},{1,17},{9,25},{17,1},{25,9},{2,18},{10... | collective-permute-start | bytes 516104 | tf_op jit(solution)/shard_map/ppermute | solution.py:11
  (68 other events, 632.7 us)
